TPU v7x, 32 devices: a whole 2x2x4 slice. The times are simulated.
32 devices in a mesh: row: 4 (over z), col: 4 (over y, x), tm: 2 (over core).
Axes of the slice: x: 2, y: 2, z: 4, core: 2. Of those that a mesh axis runs over, the one named last changes fastest.
Arguments:
- g_occ: float32 [2, 6144, 6144], P('tm', 'row', 'col'), may hold values from -6 to 6
- g_emp: float32 [2, 6144, 6144], P('tm', 'row', 'col'), may hold values from -6 to 6
- basis: float32 [6144, 1024], P('col'), may hold values from -0.078125 to 0.078125
Outputs:
- spectrum: float32 [2, 1024, 1024], P('tm', 'row', 'col')
All inputs are finite; a program needn't handle non-finite values.
Results may differ from a plain program's by a relative error of at most 0.000071.
Values sent between devices are 32-bit elements; how exact they have to be, the bound alone decides.
No kernel may reach another device: no remote copies, remote signals or barrier semaphores. Data moves between devices by JAX's collectives and lax.ppermute only.
A program may use at most 128 MiB of HBM per device.

v0:
```python
import jax
import jax.numpy as jnp
from jax import lax
from jax.sharding import PartitionSpec as P

HIGHEST_PRECISION = lax.Precision.HIGHEST


def broadcast(block, axis, source):
    block = jnp.where(lax.axis_index(axis) == source, block, jnp.zeros_like(block))
    return lax.psum(block, axis)


def per_device(g_occ, g_emp, basis):
    response = g_occ[0] * g_emp[0]
    rows_dev = response.shape[0]
    cols_dev = basis.shape[0]
    first_row = lax.axis_index("row") * rows_dev
    owner = first_row // cols_dev
    offset_local = first_row % cols_dev
    mine = lax.dynamic_slice_in_dim(basis, offset_local, rows_dev, 0)
    panel = broadcast(mine, "col", owner)
    mixed = jnp.dot(
        response, basis, precision=HIGHEST_PRECISION, preferred_element_type=jnp.float32
    )
    mixed_rows = lax.psum_scatter(mixed, "col", scatter_dimension=1, tiled=True)
    projected = lax.psum_scatter(
        lax.dot_general(
            panel,
            mixed_rows,
            (((0,), (0,)), ((), ())),
            precision=HIGHEST_PRECISION,
            preferred_element_type=jnp.float32,
        ),
        "row",
        scatter_dimension=0,
        tiled=True,
    )
    points = lax.axis_size("tm")
    moment = lax.axis_index("tm").astype(jnp.float32)
    orders = jnp.arange(1 * lax.axis_size("tm"), dtype=jnp.int32).astype(jnp.float32)
    weights = jnp.sqrt(2.0 / points) * jnp.cos(jnp.pi * (orders + 0.5) * (moment + 0.5) / points)
    return lax.psum_scatter(
        weights[:, None, None] * projected[None, :, :], "tm", scatter_dimension=0, tiled=True
    )


def solution(mesh):
    return jax.shard_map(
        per_device,
        mesh=mesh,
        in_specs=(P("tm", "row", "col"), P("tm", "row", "col"), P("col", None)),
        out_specs=P("tm", "row", "col"),
        check_vma=False,
    )
```

profile of v0, /device:TPU:0, one launch (start us, length us, event | category | flops | bytes accessed | tf_op | source)
XLA Modules:
  0.0 283.3 jit_solution(11242491472990814980)
XLA Ops:
  6.5 0.0 all-reduce.2.cloned.1.call-start
  6.5 6.8 %broadcast_select_fusion = f32[1536,1024]{1,0:T(8,128)} fusion(f32[1536,1024]{1,0:T(8,128)} %param.5, pred[]{:T(512)S(6)} %eq.5), kind=kLoop, calls=%fused_computation.3 | loop fusion | flops 1572864 | bytes 12582913 | tf_op jit(solution)/shard_map/jit(_where)/select_n | solution.py:10
  13.4 0.0 all-reduce.2.cloned.1.call-update
  13.4 0.0 reduce-scatter.4.cloned.1.call-start
  13.4 36.6 %fusion = f32[1536,1024]{1,0:T(8,128)} fusion(f32[1536,1024]{1,0:T(8,128)} %param.5, f32[1,1536,1536]{2,1,0:T(8,128)} %param.3, f32[1,1536,1536]{2,1,0:T(8,128)} %param.4), kind=kOutput, calls=%fused_computation | convolution fusion | flops 28993388544 | bytes 31457280 | tf_op jit(solution)/shard_map/dot_general | solution.py:23
  50.1 0.0 reduce-scatter.4.cloned.1.call-update
  50.1 0.2 reduce-scatter.6.cloned.1.call-start
  50.3 104.1 %all-reduce.2.cloned.1.call-done = f32[1536,1024]{1,0:T(8,128)} async-done(((f32[1536,1024]{1,0:T(8,128)}), f32[1536,1024]{1,0:T(8,128)}) %all-reduce.2.cloned.1.call-update) | async-done | bytes 6291472 | tf_op jit(solution)/shard_map/psum | solution.py:11
  154.4 73.1 %reduce-scatter.4.cloned.1.call-done = f32[1536,256]{1,0:T(8,128)} async-done(((f32[1536,1024]{1,0:T(8,128)}), f32[1536,256]{1,0:T(8,128)}) %reduce-scatter.4.cloned.1.call-update) | async-done | bytes 1572880 | tf_op jit(solution)/shard_map/reduce_scatter | solution.py:26
  227.5 13.3 %fusion.3 = f32[1024,256]{1,0:T(8,128)} fusion(f32[1536,1024]{1,0:T(8,128)} %all-reduce.2.cloned.1.call-done, f32[1536,256]{1,0:T(8,128)} %reduce-scatter.4.cloned.1.call-done), kind=kOutput, calls=%fused_computation.6 | convolution fusion | flops 4831838208 | bytes 8912896 | tf_op jit(solution)/shard_map/dot_general | solution.py:28
  240.7 0.0 reduce-scatter.6.cloned.1.call-update
  240.8 0.0 reduce-scatter.8.cloned.1.call-start
  240.9 27.3 %reduce-scatter.6.cloned.1.call-done = f32[256,256]{1,0:T(8,128)} async-done(((f32[1024,256]{1,0:T(8,128)}), f32[256,256]{1,0:T(8,128)}) %reduce-scatter.6.cloned.1.call-update) | async-done | bytes 262160 | tf_op jit(solution)/shard_map/reduce_scatter | solution.py:27
  268.2 1.8 broadcast_multiply_fusion
  270.0 0.0 reduce-scatter.8.cloned.1.call-update
  270.1 6.7 %reduce-scatter.8.cloned.1.call-done = f32[1,256,256]{2,1,0:T(8,128)} async-done(((f32[2,256,256]{2,1,0:T(8,128)}), f32[1,256,256]{2,1,0:T(8,128)}) %reduce-scatter.8.cloned.1.call-update) | async-done | bytes 262160 | tf_op jit(solution)/shard_map/reduce_scatter | solution.py:43
  (1 shorter events, 0.0 us)
Async XLA Ops:
  6.5 147.9 %all-reduce.2.cloned.1.call-start = ((), (), s32[]{:S(2)}) async-start(), calls=%async_computation.3 | async-start | bytes 12582912 | tf_op jit(solution)/shard_map/psum | solution.py:11
  13.4 214.1 %reduce-scatter.4.cloned.1.call-start = ((), (), s32[]{:S(2)}) async-start(), calls=%async_computation.4 | async-start | bytes 7864320 | tf_op jit(solution)/shard_map/reduce_scatter | solution.py:26
  50.1 218.1 %reduce-scatter.6.cloned.1.call-start = ((), (), s32[]{:S(2)}) async-start(), calls=%async_computation.5 | async-start | bytes 1310720 | tf_op jit(solution)/shard_map/reduce_scatter | solution.py:27
  240.8 36.0 %reduce-scatter.8.cloned.1.call-start = ((), (), s32[]{:S(2)}) async-start(), calls=%async_computation.6 | async-start | bytes 786432 | tf_op jit(solution)/shard_map/reduce_scatter | solution.py:43
Sparse Core Ops, SparseCore 0:
  13.5 140.8 all-reduce.1
  157.4 70.0 reduce-scatter.3
  240.9 27.2 reduce-scatter.5
  270.3 6.4 reduce-scatter.7
where the time goes:
time: 283 us
  waiting for transfers between devices  211 us (75%)
  matrix products  49.9 us (18%)
  between operations  13.1 us (5%)
  other arithmetic  8.7 us (3%)
    psum x1, waiting for transfers between devices, broadcast(): return lax.psum(block, axis)  104 us
    reduce_scatter x1, waiting for transfers between devices, per_device(): mixed_rows = lax.psum_scatter(mixed, 'col', scatter_dimension=1, tiled=True)  73.1 us
    dot_general x1, matrix products, per_device(): jnp.dot(response, basis, precision=HIGHEST_PRECISION, preferred_element_t...  36.6 us
    reduce_scatter x1, waiting for transfers between devices, per_device(): lax.psum_scatter(lax.dot_general(panel, mixed_rows, (((0,), (0,)), ((), (...  27.3 us
    dot_general x1, matrix products, per_device(): lax.dot_general(panel, mixed_rows, (((0,), (0,)), ((), ())), precision=HI...  13.3 us
    select_n x1, other arithmetic, broadcast(): jnp.where(lax.axis_index(axis) == source, block, jnp.zeros_like(block))  6.82 us
    reduce_scatter x1, waiting for transfers between devices, per_device(): lax.psum_scatter(weights[:, None, None] * projected[None, :, :], 'tm', sc...  6.71 us
  transfers between devices with their start and end apart: 4, of which 4 were waited for; matrix products, arithmetic and copies ran while one was open for 13% of the time, Pallas kernels for 0%

commit v1 on v0

--- a/solution.py
+++ b/solution.py
@@ -6,9 +6,15 @@
 HIGHEST_PRECISION = lax.Precision.HIGHEST
 
 
+def summed_here(x, mesh_axis):
+    parts = lax.all_gather(x, mesh_axis, axis=0, tiled=False)
+    total = parts.sum(axis=0)
+    return total
+
+
 def broadcast(block, axis, source):
     block = jnp.where(lax.axis_index(axis) == source, block, jnp.zeros_like(block))
-    return lax.psum(block, axis)
+    return summed_here(block, axis)
 
 
 def per_device(g_occ, g_emp, basis):

time: 283 us -> 373 us (1.32)
  waiting for transfers between devices: 211 us -> 288 us
  other arithmetic: 8.7 us -> 21.6 us
    all_gather x0 -> x1, waiting for transfers between devices: none -> 194 us  [summed_here(): parts = lax.all_gather(x, mesh_axis, axis=0, tiled=False)]
    psum x1 -> x0, waiting for transfers between devices: 104 us -> none  [broadcast(): return lax.psum(block, axis)]
    reduce_scatter x1, waiting for transfers between devices: 73.1 us -> 60.1 us  [per_device(): mixed_rows = lax.psum_scatter(mixed, 'col', scatter_dimension=1, tiled=True)]
    reduce_sum x0 -> x1, other arithmetic: none -> 12.9 us  [summed_here(): total = parts.sum(axis=0)]
where the time goes in v1:
time: 373 us
  waiting for transfers between devices  288 us (77%)
  matrix products  49.9 us (13%)
  other arithmetic  21.6 us (6%)
  between operations  13.1 us (4%)
    all_gather x1, waiting for transfers between devices, summed_here(): parts = lax.all_gather(x, mesh_axis, axis=0, tiled=False)  194 us
    reduce_scatter x1, waiting for transfers between devices, per_device(): mixed_rows = lax.psum_scatter(mixed, 'col', scatter_dimension=1, tiled=True)  60.1 us
    dot_general x1, matrix products, per_device(): jnp.dot(response, basis, precision=HIGHEST_PRECISION, preferred_element_t...  36.6 us
    reduce_scatter x1, waiting for transfers between devices, per_device(): lax.psum_scatter(lax.dot_general(panel, mixed_rows, (((0,), (0,)), ((), (...  27.3 us
    dot_general x1, matrix products, per_device(): lax.dot_general(panel, mixed_rows, (((0,), (0,)), ((), ())), precision=HI...  13.3 us
    reduce_sum x1, other arithmetic, summed_here(): total = parts.sum(axis=0)  12.9 us
  transfers between devices with their start and end apart: 4, of which 4 were waited for; matrix products, arithmetic and copies ran while one was open for 13% of the time, Pallas kernels for 0%

profile of v1, /device:TPU:0, one launch (start us, length us, event | category | flops | bytes accessed | tf_op | source)
XLA Modules:
  0.0 372.8 jit_solution(14354237105403860569)
XLA Ops:
  6.5 0.0 all-gather.3.cloned.1.call-start
  6.5 6.9 %broadcast_select_fusion = f32[1536,1024]{1,0:T(8,128)} fusion(f32[1536,1024]{1,0:T(8,128)} %param.5, pred[]{:T(512)S(6)} %eq.5), kind=kLoop, calls=%fused_computation.3 | loop fusion | flops 1572864 | bytes 12582913 | tf_op jit(solution)/shard_map/jit(_where)/select_n | solution.py:16
  13.4 0.0 all-gather.3.cloned.1.call-update
  13.4 0.0 reduce-scatter.4.cloned.1.call-start
  13.5 36.6 %fusion = f32[1536,1024]{1,0:T(8,128)} fusion(f32[1536,1024]{1,0:T(8,128)} %param.5, f32[1,1536,1536]{2,1,0:T(8,128)} %param.3, f32[1,1536,1536]{2,1,0:T(8,128)} %param.4), kind=kOutput, calls=%fused_computation | convolution fusion | flops 28993388544 | bytes 31457280 | tf_op jit(solution)/shard_map/dot_general | solution.py:29
  50.1 0.0 reduce-scatter.4.cloned.1.call-update
  50.1 0.2 reduce-scatter.6.cloned.1.call-start
  50.4 193.5 %all-gather.3.cloned.1.call-done = f32[6144,1024]{1,0:T(8,128)} async-done(((f32[1536,1024]{1,0:T(8,128)}), f32[6144,1024]{1,0:T(8,128)}) %all-gather.3.cloned.1.call-update) | async-done | bytes 25165840 | tf_op jit(solution)/shard_map/all_gather | solution.py:10
  243.9 12.9 %reduce_sum.9 = f32[1536,1024]{1,0:T(8,128)} reduce(f32[4,1536,1024]{2,1,0:T(8,128)} %bitcast.7, f32[]{:T(128)} %constant.37.clone.1), dimensions={0}, to_apply=%region_0.1 | reduce | flops 4718592 | bytes 31457284 | tf_op jit(solution)/shard_map/reduce_sum | solution.py:11
  256.8 60.1 %reduce-scatter.4.cloned.1.call-done = f32[1536,256]{1,0:T(8,128)} async-done(((f32[1536,1024]{1,0:T(8,128)}), f32[1536,256]{1,0:T(8,128)}) %reduce-scatter.4.cloned.1.call-update) | async-done | bytes 1572880 | tf_op jit(solution)/shard_map/reduce_scatter | solution.py:32
  316.9 13.3 %fusion.3 = f32[1024,256]{1,0:T(8,128)} fusion(f32[1536,1024]{1,0:T(8,128)} %reduce_sum.9, f32[1536,256]{1,0:T(8,128)} %reduce-scatter.4.cloned.1.call-done), kind=kOutput, calls=%fused_computation.6 | convolution fusion | flops 4831838208 | bytes 8912896 | tf_op jit(solution)/shard_map/dot_general | solution.py:34
  330.2 0.0 reduce-scatter.6.cloned.1.call-update
  330.2 0.0 reduce-scatter.8.cloned.1.call-start
  330.3 27.3 %reduce-scatter.6.cloned.1.call-done = f32[256,256]{1,0:T(8,128)} async-done(((f32[1024,256]{1,0:T(8,128)}), f32[256,256]{1,0:T(8,128)}) %reduce-scatter.6.cloned.1.call-update) | async-done | bytes 262160 | tf_op jit(solution)/shard_map/reduce_scatter | solution.py:33
  357.7 1.8 broadcast_multiply_fusion
  359.5 0.0 reduce-scatter.8.cloned.1.call-update
  359.5 6.7 %reduce-scatter.8.cloned.1.call-done = f32[1,256,256]{2,1,0:T(8,128)} async-done(((f32[2,256,256]{2,1,0:T(8,128)}), f32[1,256,256]{2,1,0:T(8,128)}) %reduce-scatter.8.cloned.1.call-update) | async-done | bytes 262160 | tf_op jit(solution)/shard_map/reduce_scatter | solution.py:49
  (1 shorter events, 0.0 us)
Async XLA Ops:
  6.5 237.3 %all-gather.3.cloned.1.call-start = ((), (), s32[]{:S(2)}) async-start(), calls=%async_computation.6 | async-start | bytes 31457280 | tf_op jit(solution)/shard_map/all_gather | solution.py:10
  13.4 303.5 %reduce-scatter.4.cloned.1.call-start = ((), (), s32[]{:S(2)}) async-start(), calls=%async_computation.3 | async-start | bytes 7864320 | tf_op jit(solution)/shard_map/reduce_scatter | solution.py:32
  50.1 307.5 %reduce-scatter.6.cloned.1.call-start = ((), (), s32[]{:S(2)}) async-start(), calls=%async_computation.4 | async-start | bytes 1310720 | tf_op jit(solution)/shard_map/reduce_scatter | solution.py:33
  330.2 36.0 %reduce-scatter.8.cloned.1.call-start = ((), (), s32[]{:S(2)}) async-start(), calls=%async_computation.5 | async-start | bytes 786432 | tf_op jit(solution)/shard_map/reduce_scatter | solution.py:49
Sparse Core Ops, SparseCore 0:
  13.5 230.2 all-gather.2
  246.9 70.0 reduce-scatter.3
  330.3 27.2 reduce-scatter.5
  359.8 6.4 reduce-scatter.7
